TPU v7x, 128 devices: a whole 4x4x4 slice. The times are simulated.
128 devices in a mesh: row: 8 (over x, y_lo), col: 8 (over z, y_hi), depth: 2 (over core).
Axes of the slice: x: 4, y: 4 (y_hi: 2, y_lo: 2; y = y_hi * 2 + y_lo), z: 4, core: 2. Of those that a mesh axis runs over, the one named last changes fastest.
Arguments:
- amplitudes: bfloat16 [20480, 20480], P('row', 'col'), may hold values from -0.109375 to 0.109375
- coulomb_vertex: bfloat16 [256, 20480], P('depth', ('row', 'col')), may hold values from -1.5 to 1.5
Outputs:
- cycle_residual: bfloat16 [20480, 20480], P('row', ('col', 'depth'))
- structure_factor: float32 [256], P('depth')
All inputs are finite; a program needn't handle non-finite values.
Results may differ from a plain program's by a relative error of at most 0.0057.
Values may be sent and summed in bfloat16 or wider, within the bound.
No kernel may reach another device: no remote copies, remote signals or barrier semaphores. Data moves between devices by JAX's collectives and lax.ppermute only.
A program may use at most 128 MiB of HBM per device.

v0:
```python
import jax
import jax.numpy as jnp
from jax import lax
from jax.sharding import PartitionSpec as P


def broadcast(array, axis, root):
    mine = lax.axis_index(axis) == root
    return lax.psum(jnp.where(mine, array, jnp.zeros_like(array)), axis)


def body(amplitudes, coulomb_vertex):
    row_index = lax.axis_index("row")
    col_index = lax.axis_index("col")
    block_width = amplitudes.shape[0]
    on_diagonal = (row_index == col_index).astype(jnp.float32)
    vertex_rows = lax.all_gather(coulomb_vertex, "col", axis=1, tiled=True)
    vertex_cols = broadcast(vertex_rows, "row", col_index)
    dressing = jnp.dot(vertex_rows, amplitudes, preferred_element_type=jnp.float32)
    factor_part = jnp.sum(dressing * vertex_cols.astype(jnp.float32), axis=1)
    structure_factor = lax.psum(factor_part, ("row", "col"))
    dressed_term = dressing + on_diagonal * vertex_rows.astype(jnp.float32)
    dressed_part = lax.psum_scatter(dressed_term, "row", scatter_dimension=1, tiled=True)
    dressed = dressed_part.astype(jnp.bfloat16)
    everything = lax.all_gather(dressed, ("row", "col"), axis=1, tiled=True)
    fields_here = everything.shape[0]
    grid_side = lax.axis_size("row")
    ordered = everything.reshape(fields_here, grid_side, grid_side, dressed.shape[1])
    ordered = jnp.transpose(ordered, (0, 2, 1, 3)).reshape(
        fields_here, grid_side * grid_side * dressed.shape[1]
    )
    dressed_cols = lax.dynamic_slice_in_dim(ordered, col_index * block_width, block_width, 1)
    dressed_rows = lax.dynamic_slice_in_dim(ordered, row_index * block_width, block_width, 1)
    cols_all = lax.all_to_all(dressed_cols, "depth", split_axis=1, concat_axis=0, tiled=True)
    rows_all = lax.all_gather(dressed_rows, "depth", axis=0, tiled=True)
    product = lax.dot_general(
        rows_all, cols_all, (((0,), (0,)), ((), ())), preferred_element_type=jnp.float32
    )
    cycle_residual = product.astype(jnp.bfloat16)
    return (cycle_residual, structure_factor)


def solution(mesh):
    return jax.shard_map(
        body,
        mesh=mesh,
        in_specs=(P("row", "col"), P("depth", ("row", "col"))),
        out_specs=(P("row", ("col", "depth")), P("depth")),
        check_vma=False,
    )
```

profile of v0, /device:TPU:1, one launch (start us, length us, event | category | flops | bytes accessed | tf_op | source)
XLA Modules:
  0.0 711.8 jit_solution(17845553352122211983)
XLA Ops:
  7.2 0.0 all-reduce.2.cloned.1.call-start
  7.2 33.1 %all_gather.9 = bf16[128,2560]{0,1:T(8,128)(2,1)S(1)} all-gather(bf16[128,320]{0,1:T(8,128)(2,1)} %param.3), channel_id=1, replica_groups=mesh['row'=8,'col'=8,'depth'=2] {'col'}, dimensions={1}, use_global_device_ids=true | all-gather | bytes 737280 | tf_op jit(solution)/shard_map/all_gather | solution.py:17
  40.3 0.2 copy.17
  40.6 0.9 broadcast_select_fusion
  41.5 0.0 all-reduce.2.cloned.1.call-update
  41.5 0.0 reduce-scatter.4.cloned.1.call-start
  41.5 77.2 %all-reduce.2.cloned.1.call-done = bf16[128,2560]{1,0:T(8,128)(2,1)} async-done(((bf16[128,2560]{1,0:T(8,128)(2,1)}), bf16[128,2560]{1,0:T(8,128)(2,1)}) %all-reduce.2.cloned.1.call-update) | async-done | bytes 655376 | tf_op jit(solution)/shard_map/psum | solution.py:9
  118.7 6.9 multiply_reduce_fusion
  125.6 1.5 copy.22
  127.1 0.0 reduce-scatter.4.cloned.1.call-update
  127.1 0.0 all-gather.3.cloned.1.call-start
  127.1 42.3 %reduce-scatter.4.cloned.1.call-done = f32[320,128]{1,0:T(8,128)} async-done(((f32[2560,128]{1,0:T(8,128)}), f32[320,128]{1,0:T(8,128)}) %reduce-scatter.4.cloned.1.call-update) | async-done | bytes 163856
  169.5 1.6 bitcast_convert_fusion
  171.0 0.0 all-gather.3.cloned.1.call-update
  171.1 0.0 all-gather.5.cloned.1.call-start
  171.1 301.0 %all-gather.3.cloned.1.call-done = bf16[128,20480]{0,1:T(8,128)(2,1)} async-done(((bf16[128,320]{0,1:T(8,128)(2,1)}), bf16[128,20480]{0,1:T(8,128)(2,1)}) %all-gather.3.cloned.1.call-update) | async-done | bytes 5242896 | tf_op jit(solution)/shard_map/all_gather | solution.py:25
  472.2 2.9 copy.19
  475.1 0.9 constant_dynamic-slice_fusion
  476.0 0.0 all-gather.5.cloned.1.call-update
  476.1 148.3 %psum.15 = f32[128]{0:T(128)} all-reduce(f32[128]{0:T(128)S(1)} %get-tuple-element.4), channel_id=1, replica_groups=mesh['row'=8,'col'=8,'depth'=2] {'row','col'}, use_global_device_ids=true, to_apply=%region_3.4 | all-reduce | flops 128 | bytes 1024 | tf_op jit(solution)/shard_map/psum | solution.py:21
  624.3 74.7 %all_to_all.19 = bf16[128,2,1280]{0,2,1:T(8,128)(2,1)S(1)} all-to-all(bf16[128,2,1280]{0,2,1:T(8,128)(2,1)S(1)} %bitcast.19), channel_id=1, replica_groups=mesh['row'=8,'col'=8,'depth'=2] {'depth'}, dimensions={1} | all-to-all | bytes 1310720 | tf_op jit(solution)/shard_map/all_to_all | solution.py:34
  699.0 0.2 copy.20
  699.3 0.0 all-gather.5.cloned.1.call-done
  699.3 6.0 convolution_convert_fusion
Async XLA Ops:
  7.2 111.5 %all-reduce.2.cloned.1.call-start = ((), (), s32[]{:S(2)}) async-start(), calls=%async_computation.4 | async-start | bytes 1310720 | tf_op jit(solution)/shard_map/psum | solution.py:9
  41.5 128.0 %reduce-scatter.4.cloned.1.call-start = ((), (), s32[]{:S(2)}) async-start(), calls=%async_computation.5 | async-start | bytes 1474560
  127.1 345.1 %all-gather.3.cloned.1.call-start = ((), (), s32[]{:S(2)}) async-start(), calls=%async_computation.2 | async-start | bytes 5324800 | tf_op jit(solution)/shard_map/all_gather | solution.py:25
  171.1 528.3 %all-gather.5.cloned.1.call-start = ((), (), s32[]{:S(2)}) async-start(), calls=%async_computation.3 | async-start | bytes 1966080 | tf_op jit(solution)/shard_map/all_gather | solution.py:35
Sparse Core Ops, SparseCore 0:
  41.6 77.0 all-reduce.1
  127.2 42.2 reduce-scatter.3
  171.7 300.4 all-gather.2
  476.2 51.9 all-gather.4
where the time goes:
time: 712 us
  waiting for transfers between devices  421 us (59%)
  blocking collectives  256 us (36%)
  between operations  13.8 us (2%)
  matrix products  12.9 us (2%)
    all_gather x1, waiting for transfers between devices, body(): everything = lax.all_gather(dressed, ('row', 'col'), axis=1, tiled=True)  301 us
    psum x1, blocking collectives, body(): structure_factor = lax.psum(factor_part, ('row', 'col'))  148 us
    psum x1, waiting for transfers between devices, broadcast(): return lax.psum(jnp.where(mine, array, jnp.zeros_like(array)), axis)  77.2 us
    all_to_all x1, blocking collectives, body(): lax.all_to_all(dressed_cols, 'depth', split_axis=1, concat_axis=0, tiled=...  74.7 us
    unnamed x5, waiting for transfers between devices  42.4 us
    all_gather x1, blocking collectives, body(): vertex_rows = lax.all_gather(coulomb_vertex, 'col', axis=1, tiled=True)  33.1 us
  transfers between devices with their start and end apart: 4, of which 3 were waited for; matrix products, arithmetic and copies ran while one was open for 0% of the time, Pallas kernels for 0%

commit v1 on v0

--- a/solution.py
+++ b/solution.py
@@ -1,7 +1,17 @@
+import functools
 import jax
 import jax.numpy as jnp
 from jax import lax
 from jax.sharding import PartitionSpec as P
+
+
+def _make_sizes(my_data, ax_name, a_name):
+    piece_out = lax.psum(my_data, axis_name=ax_name)
+    current_block = lax.psum(piece_out, axis_name=a_name)
+    return current_block
+
+
+slabs_enter = functools.partial(_make_sizes, ax_name="col", a_name="row")
 
 
 def broadcast(array, axis, root):
@@ -18,7 +28,7 @@
     vertex_cols = broadcast(vertex_rows, "row", col_index)
     dressing = jnp.dot(vertex_rows, amplitudes, preferred_element_type=jnp.float32)
     factor_part = jnp.sum(dressing * vertex_cols.astype(jnp.float32), axis=1)
-    structure_factor = lax.psum(factor_part, ("row", "col"))
+    structure_factor = slabs_enter(factor_part)
     dressed_term = dressing + on_diagonal * vertex_rows.astype(jnp.float32)
     dressed_part = lax.psum_scatter(dressed_term, "row", scatter_dimension=1, tiled=True)
     dressed = dressed_part.astype(jnp.bfloat16)

time: 712 us -> 576 us (0.81)
  blocking collectives: 256 us -> 120 us
    psum x1 -> x2, blocking collectives: 148 us -> 33.1 us  [the longest x1 16.7 us: _make_sizes(): current_block = lax.psum(piece_out, axis_name=a_name)]
    all_to_all x1, blocking collectives: 74.7 us -> 54 us  [body(): lax.all_to_all(dressed_cols, 'depth', split_axis=1, concat_axis=0, tiled=...]
where the time goes in v1:
time: 576 us
  waiting for transfers between devices  421 us (73%)
  blocking collectives  120 us (21%)
  between operations  13.8 us (2%)
  matrix products  12.9 us (2%)
  local copies, waits for them, and re-layouts  5.82 us (1%)
    all_gather x1, waiting for transfers between devices, body(): everything = lax.all_gather(dressed, ('row', 'col'), axis=1, tiled=True)  301 us
    psum x1, waiting for transfers between devices, broadcast(): return lax.psum(jnp.where(mine, array, jnp.zeros_like(array)), axis)  77.2 us
    all_to_all x1, blocking collectives, body(): lax.all_to_all(dressed_cols, 'depth', split_axis=1, concat_axis=0, tiled=...  54 us
    unnamed x5, waiting for transfers between devices  42.4 us
    all_gather x1, blocking collectives, body(): vertex_rows = lax.all_gather(coulomb_vertex, 'col', axis=1, tiled=True)  33.1 us
    psum x1, blocking collectives, _make_sizes(): current_block = lax.psum(piece_out, axis_name=a_name)  16.7 us
    psum x1, blocking collectives, _make_sizes(): piece_out = lax.psum(my_data, axis_name=ax_name)  16.4 us
  transfers between devices with their start and end apart: 4, of which 3 were waited for; matrix products, arithmetic and copies ran while one was open for 0% of the time, Pallas kernels for 0%

profile of v1, /device:TPU:1, one launch (start us, length us, event | category | flops | bytes accessed | tf_op | source)
XLA Modules:
  0.0 575.9 jit_solution(15061622711367103999)
XLA Ops:
  7.2 0.0 all-reduce.2.cloned.1.call-start
  7.2 33.1 %all_gather.9 = bf16[128,2560]{0,1:T(8,128)(2,1)S(1)} all-gather(bf16[128,320]{0,1:T(8,128)(2,1)} %param.3), channel_id=1, replica_groups=mesh['row'=8,'col'=8,'depth'=2] {'col'}, dimensions={1}, use_global_device_ids=true | all-gather | bytes 737280 | tf_op jit(solution)/shard_map/all_gather | solution.py:27
  40.3 0.2 copy.17
  40.6 0.9 broadcast_select_fusion
  41.5 0.0 all-reduce.2.cloned.1.call-update
  41.5 0.0 reduce-scatter.4.cloned.1.call-start
  41.5 77.2 %all-reduce.2.cloned.1.call-done = bf16[128,2560]{1,0:T(8,128)(2,1)} async-done(((bf16[128,2560]{1,0:T(8,128)(2,1)}), bf16[128,2560]{1,0:T(8,128)(2,1)}) %all-reduce.2.cloned.1.call-update) | async-done | bytes 655376 | tf_op jit(solution)/shard_map/psum | solution.py:19
  118.7 6.9 %multiply_reduce_fusion = (f32[128]{0:T(128)S(1)}, f32[128,2560]{1,0:T(8,128)S(1)}) fusion(bf16[128,2560]{1,0:T(8,128)(2,1)} %all-reduce.2.cloned.1.call-done, bf16[128,2560]{1,0:T(8,128)(2,1)S(1)} %copy.17, f32[]{:T(128)S(6)} %convert_element_type.15, bf16[128,2560]{0,1:T(8,128)(2,1)S(1)} %all_gather.9, bf16[2560,2560]{1,0:T(8,128)(2,1)} %param.2), kind=kOutput, calls=%fused_computation.1 | convolution fusion | flops 1679687552 | bytes 16384516 | tf_op jit(solution)/shard_map/dot_general | solution.py:29
  125.6 1.5 copy.22
  127.1 0.0 reduce-scatter.4.cloned.1.call-update
  127.1 0.0 all-gather.3.cloned.1.call-start
  127.1 42.3 %reduce-scatter.4.cloned.1.call-done = f32[320,128]{1,0:T(8,128)} async-done(((f32[2560,128]{1,0:T(8,128)}), f32[320,128]{1,0:T(8,128)}) %reduce-scatter.4.cloned.1.call-update) | async-done | bytes 163856
  169.5 1.6 bitcast_convert_fusion
  171.0 0.0 all-gather.3.cloned.1.call-update
  171.1 0.0 all-gather.5.cloned.1.call-start
  171.1 301.0 %all-gather.3.cloned.1.call-done = bf16[128,20480]{0,1:T(8,128)(2,1)} async-done(((bf16[128,320]{0,1:T(8,128)(2,1)}), bf16[128,20480]{0,1:T(8,128)(2,1)}) %all-gather.3.cloned.1.call-update) | async-done | bytes 5242896 | tf_op jit(solution)/shard_map/all_gather | solution.py:35
  472.2 2.9 copy.19
  475.1 0.9 constant_dynamic-slice_fusion
  476.0 0.0 all-gather.5.cloned.1.call-update
  476.1 16.4 %psum.22 = f32[128]{0:T(128)S(1)} all-reduce(f32[128]{0:T(128)S(1)} %get-tuple-element.4), channel_id=1, replica_groups=mesh['row'=8,'col'=8,'depth'=2] {'col'}, use_global_device_ids=true, to_apply=%region_3.4 | all-reduce | flops 128 | bytes 1024 | tf_op jit(solution)/shard_map/psum | solution.py:9
  492.4 16.7 %psum.23 = f32[128]{0:T(128)} all-reduce(f32[128]{0:T(128)S(1)} %psum.22), channel_id=1, replica_groups=mesh['row'=8,'col'=8,'depth'=2] {'row'}, use_global_device_ids=true, to_apply=%region_4.5 | all-reduce | flops 128 | bytes 1024 | tf_op jit(solution)/shard_map/psum | solution.py:10
  509.2 54.0 %all_to_all.19 = bf16[128,2,1280]{0,2,1:T(8,128)(2,1)S(1)} all-to-all(bf16[128,2,1280]{0,2,1:T(8,128)(2,1)S(1)} %bitcast.19), channel_id=1, replica_groups=mesh['row'=8,'col'=8,'depth'=2] {'depth'}, dimensions={1} | all-to-all | bytes 1310720 | tf_op jit(solution)/shard_map/all_to_all | solution.py:44
  563.1 0.2 copy.20
  563.4 0.0 all-gather.5.cloned.1.call-done
  563.4 6.0 %convolution_convert_fusion = bf16[2560,1280]{1,0:T(8,128)(2,1)} fusion(bf16[256,2560]{0,1:T(8,128)(2,1)} %all-gather.5.cloned.1.call-done, bf16[256,1280]{1,0:T(8,128)(2,1)S(1)} %bitcast.17), kind=kOutput, calls=%fused_computation | convolution fusion | flops 1680998400 | bytes 8519680 | tf_op jit(solution)/shard_map/dot_general | solution.py:46
Async XLA Ops:
  7.2 111.5 %all-reduce.2.cloned.1.call-start = ((), (), s32[]{:S(2)}) async-start(), calls=%async_computation.4 | async-start | bytes 1310720 | tf_op jit(solution)/shard_map/psum | solution.py:19
  41.5 128.0 %reduce-scatter.4.cloned.1.call-start = ((), (), s32[]{:S(2)}) async-start(), calls=%async_computation.5 | async-start | bytes 1474560
  127.1 345.1 %all-gather.3.cloned.1.call-start = ((), (), s32[]{:S(2)}) async-start(), calls=%async_computation.2 | async-start | bytes 5324800 | tf_op jit(solution)/shard_map/all_gather | solution.py:35
  171.1 392.3 %all-gather.5.cloned.1.call-start = ((), (), s32[]{:S(2)}) async-start(), calls=%async_computation.3 | async-start | bytes 1966080 | tf_op jit(solution)/shard_map/all_gather | solution.py:45
Sparse Core Ops, SparseCore 0:
  41.6 77.0 all-reduce.1
  127.2 42.2 reduce-scatter.3
  171.7 300.4 all-gather.2
  476.2 51.8 all-gather.4
